TPU v7x, 32 devices: a whole 2x2x4 slice. The times are simulated.
32 devices in a mesh: groups: 2 (over x), blk: 16 (over z, y, core).
Axes of the slice: x: 2, y: 2, z: 4, core: 2. Of those that a mesh axis runs over, the one named last changes fastest.
Arguments:
- queries: bfloat16 [32, 8192], P(('groups', 'blk')), parts along dimension 0, may hold values from -100 to 100
- prefix_key_value: bfloat16 [2, 32768, 1024], P(None, ('groups', 'blk')), parts along dimension 1, may hold values from -7 to 7
- suffix_key_value: bfloat16 [32, 2, 512, 1024], P(('groups', 'blk')), parts along dimension 0, may hold values from -9 to 9
- fresh_key_value: bfloat16 [32, 2, 1024], P(('groups', 'blk')), parts along dimension 0, may hold values from -9 to 9
- lengths: int32 [32], P('groups'), parts along dimension 0, may hold values from 1 to 512, 4096 in all
- home: int32 [32], P('groups'), parts along dimension 0, may hold values from 0 to 15, each once
Outputs:
- attended: bfloat16 [32, 8192], P(('groups', 'blk')), parts along dimension 0
There are 2 independent parts, one for each index of `groups`. A program takes and returns all parts, laid end to end along the dimension named above; each array names one. Nothing has to cross between parts.
Inputs may be any that keep to these rules, and one draw needn't show every extreme that they name: Row r's suffix cache lies in slot home[r]; every slot holds exactly one row. `lengths`: some row has exactly 512 suffix tokens.
All inputs are finite; a program needn't handle non-finite values.
Results may differ from a plain program's by a relative error of at most 0.0049.
Values may be sent and summed in bfloat16 or wider, within the bound.
No kernel may reach another device: no remote copies, remote signals or barrier semaphores. Data moves between devices by JAX's collectives and lax.ppermute only.
A program may use at most 128 MiB of HBM per device.

v0:
```python
import jax
import jax.numpy as jnp
from jax import lax
from jax.sharding import PartitionSpec as P

QUERY_HEADS = 64
KEY_VALUE_HEADS = 8
HEAD_WIDTH = 128


def per_device(queries, prefix_key_value, suffix_key_value, fresh_key_value, lengths, home):
    rows_per_block = queries.shape[0]
    blocks = lax.axis_size("blk")
    my_index = lax.axis_index("blk")
    revision_count = rows_per_block * blocks
    query_group = QUERY_HEADS // KEY_VALUE_HEADS
    score_scale = HEAD_WIDTH ** (-0.5)
    prefix_length_count = prefix_key_value.shape[1]
    suffix_length_count = suffix_key_value.shape[2]
    gathered_parts = lax.all_gather(queries, "blk", axis=0, tiled=True)
    grouped_queries = gathered_parts.reshape(
        revision_count, KEY_VALUE_HEADS, query_group, HEAD_WIDTH
    )
    query_head_rows = grouped_queries.transpose(1, 0, 2, 3).reshape(
        KEY_VALUE_HEADS, revision_count * query_group, HEAD_WIDTH
    )
    key_head_rows = (
        prefix_key_value[0]
        .reshape(prefix_length_count, KEY_VALUE_HEADS, HEAD_WIDTH)
        .transpose(1, 0, 2)
    )
    value_head_rows = (
        prefix_key_value[1]
        .reshape(prefix_length_count, KEY_VALUE_HEADS, HEAD_WIDTH)
        .transpose(1, 0, 2)
    )

    def prefix_head(item):
        query_block, keys_block, values_block = item
        scores = (
            jnp.dot(query_block, keys_block.T, preferred_element_type=jnp.float32) * score_scale
        )
        peak = jnp.max(scores, axis=-1)
        exponent = jnp.exp(scores - peak[:, None])
        totals = jnp.sum(exponent, axis=-1)
        accum = jnp.dot(
            exponent.astype(jnp.bfloat16), values_block, preferred_element_type=jnp.float32
        )
        return (peak, totals, accum)

    prefix_score_peak, prefix_weight_sum, prefix_accum_sum = lax.map(
        prefix_head, (query_head_rows, key_head_rows, value_head_rows)
    )
    prefix_score_peak = prefix_score_peak.reshape(
        KEY_VALUE_HEADS, revision_count, query_group
    ).transpose(1, 0, 2)
    prefix_weight_sum = prefix_weight_sum.reshape(
        KEY_VALUE_HEADS, revision_count, query_group
    ).transpose(1, 0, 2)
    prefix_accum_sum = prefix_accum_sum.reshape(
        KEY_VALUE_HEADS, revision_count, query_group, HEAD_WIDTH
    ).transpose(1, 0, 2, 3)
    slot_ids = my_index * rows_per_block + jnp.arange(rows_per_block, dtype=jnp.int32)
    row_ids = jnp.arange(revision_count, dtype=jnp.int32)
    matches = home[None, :] == slot_ids[:, None]
    row_lookup = jnp.sum(jnp.where(matches, row_ids[None, :], 0), axis=1)
    slot_queries = grouped_queries[row_lookup]
    slot_key_rows = suffix_key_value[:, 0].reshape(
        rows_per_block, suffix_length_count, KEY_VALUE_HEADS, HEAD_WIDTH
    )
    slot_value_rows = suffix_key_value[:, 1].reshape(
        rows_per_block, suffix_length_count, KEY_VALUE_HEADS, HEAD_WIDTH
    )
    scores = (
        jnp.einsum(
            "rhgd,rthd->rhgt", slot_queries, slot_key_rows, preferred_element_type=jnp.float32
        )
        * score_scale
    )
    live_mask = (
        jnp.arange(suffix_length_count, dtype=jnp.int32)[None, :] < lengths[row_lookup][:, None]
    )
    scores = jnp.where(live_mask[:, None, None, :], scores, -jnp.inf)
    slot_score_peak = jnp.max(scores, axis=-1)
    exponent = jnp.exp(scores - slot_score_peak[..., None])
    slot_weight_sum = jnp.sum(exponent, axis=-1)
    slot_accum_sum = jnp.einsum(
        "rhgt,rthd->rhgd",
        exponent.astype(jnp.bfloat16),
        slot_value_rows,
        preferred_element_type=jnp.float32,
    )
    suffix_score_peak = (
        jnp.full((revision_count, KEY_VALUE_HEADS, query_group), -jnp.inf, jnp.float32)
        .at[row_lookup]
        .set(slot_score_peak)
    )
    suffix_weight_sum = (
        jnp.zeros((revision_count, KEY_VALUE_HEADS, query_group), jnp.float32)
        .at[row_lookup]
        .set(slot_weight_sum)
    )
    suffix_accum_sum = (
        jnp.zeros((revision_count, KEY_VALUE_HEADS, query_group, HEAD_WIDTH), jnp.float32)
        .at[row_lookup]
        .set(slot_accum_sum)
    )
    local_query_rows = queries.reshape(rows_per_block, KEY_VALUE_HEADS, query_group, HEAD_WIDTH)
    fresh_token_keys = fresh_key_value[:, 0].reshape(rows_per_block, KEY_VALUE_HEADS, HEAD_WIDTH)
    fresh_token_values = (
        fresh_key_value[:, 1]
        .reshape(rows_per_block, KEY_VALUE_HEADS, HEAD_WIDTH)
        .astype(jnp.float32)
    )
    local_score_peak = (
        jnp.einsum(
            "rhgd,rhd->rhg", local_query_rows, fresh_token_keys, preferred_element_type=jnp.float32
        )
        * score_scale
    )
    local_accum_sum = jnp.broadcast_to(
        fresh_token_values[:, :, None, :],
        (rows_per_block, KEY_VALUE_HEADS, query_group, HEAD_WIDTH),
    )
    start_offset = my_index * rows_per_block
    new_peak = lax.dynamic_update_slice_in_dim(
        jnp.full((revision_count, KEY_VALUE_HEADS, query_group), -jnp.inf, jnp.float32),
        local_score_peak,
        start_offset,
        0,
    )
    new_total = lax.dynamic_update_slice_in_dim(
        jnp.zeros((revision_count, KEY_VALUE_HEADS, query_group), jnp.float32),
        jnp.ones_like(local_score_peak),
        start_offset,
        0,
    )
    fresh_token_accum = lax.dynamic_update_slice_in_dim(
        jnp.zeros((revision_count, KEY_VALUE_HEADS, query_group, HEAD_WIDTH), jnp.float32),
        local_accum_sum,
        start_offset,
        0,
    )
    peak = jnp.maximum(prefix_score_peak, jnp.maximum(suffix_score_peak, new_peak))
    pre_fac = jnp.exp(prefix_score_peak - peak)
    suf_fac = jnp.exp(suffix_score_peak - peak)
    new_fac = jnp.exp(new_peak - peak)
    totals = pre_fac * prefix_weight_sum + suf_fac * suffix_weight_sum + new_fac * new_total
    accum = (
        pre_fac[..., None] * prefix_accum_sum
        + suf_fac[..., None] * suffix_accum_sum
        + new_fac[..., None] * fresh_token_accum
    )
    normed_half = (
        (accum / totals[..., None])
        .astype(jnp.bfloat16)
        .reshape(revision_count, QUERY_HEADS * HEAD_WIDTH)
    )
    lse = (peak + jnp.log(totals)).reshape(revision_count, QUERY_HEADS)
    landed = lax.all_to_all(
        normed_half.reshape(blocks, rows_per_block, QUERY_HEADS * HEAD_WIDTH),
        "blk",
        split_axis=0,
        concat_axis=0,
        tiled=True,
    )
    landed_lse = lax.all_to_all(
        lse.reshape(blocks, rows_per_block, QUERY_HEADS),
        "blk",
        split_axis=0,
        concat_axis=0,
        tiled=True,
    )
    highest = jnp.max(landed_lse, axis=0)
    weights = jnp.exp(landed_lse - highest[None])
    landed = landed.astype(jnp.float32).reshape(blocks, rows_per_block, QUERY_HEADS, HEAD_WIDTH)
    numerator = jnp.sum(weights[..., None] * landed, axis=0)
    denominator = jnp.sum(weights, axis=0)
    result = numerator / denominator[..., None]
    return result.reshape(rows_per_block, QUERY_HEADS * HEAD_WIDTH).astype(jnp.bfloat16)


def solution(mesh):
    placed = (
        P(("groups", "blk"), None),
        P(None, ("groups", "blk"), None),
        P(("groups", "blk"), None, None, None),
        P(("groups", "blk"), None, None),
        P("groups"),
        P("groups"),
    )
    return jax.shard_map(
        per_device,
        mesh=mesh,
        in_specs=placed,
        out_specs=P(("groups", "blk"), None),
        check_vma=False,
    )
```

profile of v0, /device:TPU:0, one launch (start us, length us, event | category | flops | bytes accessed | tf_op | source)
XLA Modules:
  0.0 108.4 jit_solution(14778481534086391625)
XLA Ops:
  0.0 1.3 %fusion.34 = s32[]{:T(128)} fusion(s32[16]{0:T(128)} %param.19, s32[]{:T(128)S(6)} %axis_index.12), kind=kLoop, calls=%fused_computation.58 | loop fusion | flops 47 | bytes 72 | tf_op jit(solution)/shard_map/reduce_sum | solution.py:66
  3.2 1.2 %dynamic-slice.24 = s32[1]{0:T(128)} dynamic-slice(s32[16]{0:T(128)} %param.18, s32[]{:T(128)} %bitcast.15), dynamic_slice_sizes={1} | dynamic-slice | bytes 12 | tf_op jit(solution)/shard_map/gather | solution.py:81
  4.5 1.1 %iota_compare_fusion = pred[512]{0:T(512)(128)(4,1)} fusion(s32[]{:T(128)} %bitcast.16), kind=kLoop, calls=%fused_computation.53 | loop fusion | flops 512 | bytes 516 | tf_op jit(solution)/shard_map/lt | solution.py:81
  5.6 1.7 %fusion.40 = (bf16[1,1,512,1024]{3,2,1,0:T(8,128)(2,1)S(1)}, bf16[1,1,512,1024]{3,2,1,0:T(8,128)(2,1)S(1)}) fusion(bf16[1,2,512,1024]{3,2,1,0:T(8,128)(2,1)} %param.16), kind=kLoop, calls=%fused_computation.62 | loop fusion | bytes 4194304 | tf_op jit(solution)/shard_map/slice | solution.py:71
  7.4 0.5 copy.117
  8.1 24.6 %all-gather = bf16[16,1,8192]{2,1,0:T(2,128)(2,1)S(1)} all-gather(bf16[1,1,8192]{2,1,0:T(2,128)(2,1)S(1)} %bitcast.126), channel_id=1, replica_groups=mesh['groups'=2,'blk'=16] {'blk'}, dimensions={0}, use_global_device_ids=true | all-gather | bytes 278528 | tf_op jit(solution)/shard_map/all_gather | solution.py:20
  32.8 1.5 %reduce.26 = bf16[16,8192]{1,0:T(8,128)(2,1)S(1)} reduce(bf16[16,1,8192]{2,1,0:T(2,128)(2,1)S(1)} %all-gather, bf16[]{:T(256)} %constant.147), dimensions={1}, to_apply=%all-gather.reduce_sub_computation | reduce | bytes 524290 | tf_op jit(solution)/shard_map/all_gather | solution.py:20
  34.4 0.7 and_reduce_fusion.1
  35.1 0.9 fusion.41
  36.1 0.7 select_bitcast_fusion
  36.8 0.7 copy.96
  37.5 0.7 copy.99
  38.4 0.7 copy.97
  39.1 4.0 %fusion.39 = (bf16[1,1024,1024]{2,1,0:T(8,128)(2,1)S(1)}, bf16[1,1024,1024]{2,1,0:T(8,128)(2,1)}) fusion(bf16[2,1024,1024]{2,1,0:T(8,128)(2,1)} %param.15), kind=kLoop, calls=%fused_computation.61 | loop fusion | bytes 8388608 | tf_op jit(solution)/shard_map/slice | solution.py:33
  43.1 4.0 %copy.115 = bf16[1,1024,1024]{1,2,0:T(8,128)(2,1)} copy(bf16[1,1024,1024]{2,1,0:T(8,128)(2,1)} %get-tuple-element.164) | data formatting | bytes 4194304
  47.0 2.6 %copy.116 = bf16[1,1024,1024]{1,2,0:T(8,128)(2,1)} copy(bf16[1,1024,1024]{2,1,0:T(8,128)(2,1)S(1)} %get-tuple-element.163) | data formatting | bytes 4194304
  49.7 27.4 %while.19 = (s32[]{:T(128)}, f32[8,128]{1,0:T(8,128)S(1)}, f32[8,128]{1,0:T(8,128)S(1)}, f32[8,128,128]{2,1,0:T(8,128)}, bf16[8,128,128]{2,1,0:T(8,128)(2,1)S(1)...) while((s32[]{:T(128)}, f32[8,128]{1,0:T(8,128)S(1)}, ...), condition=%wide.region_3.4_spmd, body=%wide.region_0.3_spmd.sunk | while | flops 67895040 | bytes 2201701 | solution.py:51
  49.7 1.2 %fusion.52 = (f32[128]{0:T(128)S(1)}, f32[128,1024]{1,0:T(8,128)S(1)}) fusion(bf16[8,1024,128]{1,2,0:T(8,128)(2,1)} %get-tuple-element.241, s32[]{:T(128)} %get-tuple-element.227, bf16[8,128,128]{2,1,0:T(8,128)(2,1)S(1)} %get-tuple-element.240), kind=kOutput, calls=%fused_computation.60.clone.1 | convolution fusion | flops 33816448 | bytes 820736 | tf_op jit(solution)/shard_map/while/body/eval_jaxpr/dot_general | solution.py:41
  51.0 1.9 %fusion.54 = f32[8,128,128]{2,1,0:T(8,128)} fusion(f32[8,128,128]{2,1,0:T(8,128)} %get-tuple-element.230, s32[]{:T(128)} %get-tuple-element.227, f32[128,1024]{1,0:T(8,128)S(1)} %get-tuple-element.217, bf16[8,1024,128]{1,2,0:T(8,128)(2,1)} %get-tuple-element.242, f32[128]{0:T(128)S(1)} %get-tuple-element.216), kind=kOutput, calls=%fused_computation.2.clone.1 | convolution fusion | flops 33816576 | bytes 853504 | tf_op jit(solution)/shard_map/while/body/eval_jaxpr/dot_general | solution.py:46
  53.2 1.2 %fusion.52 = (f32[128]{0:T(128)S(1)}, f32[128,1024]{1,0:T(8,128)S(1)}) fusion(bf16[8,1024,128]{1,2,0:T(8,128)(2,1)} %get-tuple-element.241, s32[]{:T(128)} %get-tuple-element.227, bf16[8,128,128]{2,1,0:T(8,128)(2,1)S(1)} %get-tuple-element.240), kind=kOutput, calls=%fused_computation.60.clone.1 | convolution fusion | flops 33816448 | bytes 820736 | tf_op jit(solution)/shard_map/while/body/eval_jaxpr/dot_general | solution.py:41
  54.4 1.9 %fusion.54 = f32[8,128,128]{2,1,0:T(8,128)} fusion(f32[8,128,128]{2,1,0:T(8,128)} %get-tuple-element.230, s32[]{:T(128)} %get-tuple-element.227, f32[128,1024]{1,0:T(8,128)S(1)} %get-tuple-element.217, bf16[8,1024,128]{1,2,0:T(8,128)(2,1)} %get-tuple-element.242, f32[128]{0:T(128)S(1)} %get-tuple-element.216), kind=kOutput, calls=%fused_computation.2.clone.1 | convolution fusion | flops 33816576 | bytes 853504 | tf_op jit(solution)/shard_map/while/body/eval_jaxpr/dot_general | solution.py:46
  56.6 1.2 %fusion.52 = (f32[128]{0:T(128)S(1)}, f32[128,1024]{1,0:T(8,128)S(1)}) fusion(bf16[8,1024,128]{1,2,0:T(8,128)(2,1)} %get-tuple-element.241, s32[]{:T(128)} %get-tuple-element.227, bf16[8,128,128]{2,1,0:T(8,128)(2,1)S(1)} %get-tuple-element.240), kind=kOutput, calls=%fused_computation.60.clone.1 | convolution fusion | flops 33816448 | bytes 820736 | tf_op jit(solution)/shard_map/while/body/eval_jaxpr/dot_general | solution.py:41
  57.8 1.9 %fusion.54 = f32[8,128,128]{2,1,0:T(8,128)} fusion(f32[8,128,128]{2,1,0:T(8,128)} %get-tuple-element.230, s32[]{:T(128)} %get-tuple-element.227, f32[128,1024]{1,0:T(8,128)S(1)} %get-tuple-element.217, bf16[8,1024,128]{1,2,0:T(8,128)(2,1)} %get-tuple-element.242, f32[128]{0:T(128)S(1)} %get-tuple-element.216), kind=kOutput, calls=%fused_computation.2.clone.1 | convolution fusion | flops 33816576 | bytes 853504 | tf_op jit(solution)/shard_map/while/body/eval_jaxpr/dot_general | solution.py:46
  60.0 1.2 %fusion.52 = (f32[128]{0:T(128)S(1)}, f32[128,1024]{1,0:T(8,128)S(1)}) fusion(bf16[8,1024,128]{1,2,0:T(8,128)(2,1)} %get-tuple-element.241, s32[]{:T(128)} %get-tuple-element.227, bf16[8,128,128]{2,1,0:T(8,128)(2,1)S(1)} %get-tuple-element.240), kind=kOutput, calls=%fused_computation.60.clone.1 | convolution fusion | flops 33816448 | bytes 820736 | tf_op jit(solution)/shard_map/while/body/eval_jaxpr/dot_general | solution.py:41
  61.3 1.9 %fusion.54 = f32[8,128,128]{2,1,0:T(8,128)} fusion(f32[8,128,128]{2,1,0:T(8,128)} %get-tuple-element.230, s32[]{:T(128)} %get-tuple-element.227, f32[128,1024]{1,0:T(8,128)S(1)} %get-tuple-element.217, bf16[8,1024,128]{1,2,0:T(8,128)(2,1)} %get-tuple-element.242, f32[128]{0:T(128)S(1)} %get-tuple-element.216), kind=kOutput, calls=%fused_computation.2.clone.1 | convolution fusion | flops 33816576 | bytes 853504 | tf_op jit(solution)/shard_map/while/body/eval_jaxpr/dot_general | solution.py:46
  63.4 1.2 %fusion.52 = (f32[128]{0:T(128)S(1)}, f32[128,1024]{1,0:T(8,128)S(1)}) fusion(bf16[8,1024,128]{1,2,0:T(8,128)(2,1)} %get-tuple-element.241, s32[]{:T(128)} %get-tuple-element.227, bf16[8,128,128]{2,1,0:T(8,128)(2,1)S(1)} %get-tuple-element.240), kind=kOutput, calls=%fused_computation.60.clone.1 | convolution fusion | flops 33816448 | bytes 820736 | tf_op jit(solution)/shard_map/while/body/eval_jaxpr/dot_general | solution.py:41
  64.7 1.9 %fusion.54 = f32[8,128,128]{2,1,0:T(8,128)} fusion(f32[8,128,128]{2,1,0:T(8,128)} %get-tuple-element.230, s32[]{:T(128)} %get-tuple-element.227, f32[128,1024]{1,0:T(8,128)S(1)} %get-tuple-element.217, bf16[8,1024,128]{1,2,0:T(8,128)(2,1)} %get-tuple-element.242, f32[128]{0:T(128)S(1)} %get-tuple-element.216), kind=kOutput, calls=%fused_computation.2.clone.1 | convolution fusion | flops 33816576 | bytes 853504 | tf_op jit(solution)/shard_map/while/body/eval_jaxpr/dot_general | solution.py:46
  66.9 1.2 %fusion.52 = (f32[128]{0:T(128)S(1)}, f32[128,1024]{1,0:T(8,128)S(1)}) fusion(bf16[8,1024,128]{1,2,0:T(8,128)(2,1)} %get-tuple-element.241, s32[]{:T(128)} %get-tuple-element.227, bf16[8,128,128]{2,1,0:T(8,128)(2,1)S(1)} %get-tuple-element.240), kind=kOutput, calls=%fused_computation.60.clone.1 | convolution fusion | flops 33816448 | bytes 820736 | tf_op jit(solution)/shard_map/while/body/eval_jaxpr/dot_general | solution.py:41
  68.1 1.9 %fusion.54 = f32[8,128,128]{2,1,0:T(8,128)} fusion(f32[8,128,128]{2,1,0:T(8,128)} %get-tuple-element.230, s32[]{:T(128)} %get-tuple-element.227, f32[128,1024]{1,0:T(8,128)S(1)} %get-tuple-element.217, bf16[8,1024,128]{1,2,0:T(8,128)(2,1)} %get-tuple-element.242, f32[128]{0:T(128)S(1)} %get-tuple-element.216), kind=kOutput, calls=%fused_computation.2.clone.1 | convolution fusion | flops 33816576 | bytes 853504 | tf_op jit(solution)/shard_map/while/body/eval_jaxpr/dot_general | solution.py:46
  70.3 1.2 %fusion.52 = (f32[128]{0:T(128)S(1)}, f32[128,1024]{1,0:T(8,128)S(1)}) fusion(bf16[8,1024,128]{1,2,0:T(8,128)(2,1)} %get-tuple-element.241, s32[]{:T(128)} %get-tuple-element.227, bf16[8,128,128]{2,1,0:T(8,128)(2,1)S(1)} %get-tuple-element.240), kind=kOutput, calls=%fused_computation.60.clone.1 | convolution fusion | flops 33816448 | bytes 820736 | tf_op jit(solution)/shard_map/while/body/eval_jaxpr/dot_general | solution.py:41
  71.5 1.9 %fusion.54 = f32[8,128,128]{2,1,0:T(8,128)} fusion(f32[8,128,128]{2,1,0:T(8,128)} %get-tuple-element.230, s32[]{:T(128)} %get-tuple-element.227, f32[128,1024]{1,0:T(8,128)S(1)} %get-tuple-element.217, bf16[8,1024,128]{1,2,0:T(8,128)(2,1)} %get-tuple-element.242, f32[128]{0:T(128)S(1)} %get-tuple-element.216), kind=kOutput, calls=%fused_computation.2.clone.1 | convolution fusion | flops 33816576 | bytes 853504 | tf_op jit(solution)/shard_map/while/body/eval_jaxpr/dot_general | solution.py:46
  73.7 1.2 %fusion.52 = (f32[128]{0:T(128)S(1)}, f32[128,1024]{1,0:T(8,128)S(1)}) fusion(bf16[8,1024,128]{1,2,0:T(8,128)(2,1)} %get-tuple-element.241, s32[]{:T(128)} %get-tuple-element.227, bf16[8,128,128]{2,1,0:T(8,128)(2,1)S(1)} %get-tuple-element.240), kind=kOutput, calls=%fused_computation.60.clone.1 | convolution fusion | flops 33816448 | bytes 820736 | tf_op jit(solution)/shard_map/while/body/eval_jaxpr/dot_general | solution.py:41
  75.0 1.9 %fusion.54 = f32[8,128,128]{2,1,0:T(8,128)} fusion(f32[8,128,128]{2,1,0:T(8,128)} %get-tuple-element.230, s32[]{:T(128)} %get-tuple-element.227, f32[128,1024]{1,0:T(8,128)S(1)} %get-tuple-element.217, bf16[8,1024,128]{1,2,0:T(8,128)(2,1)} %get-tuple-element.242, f32[128]{0:T(128)S(1)} %get-tuple-element.216), kind=kOutput, calls=%fused_computation.2.clone.1 | convolution fusion | flops 33816576 | bytes 853504 | tf_op jit(solution)/shard_map/while/body/eval_jaxpr/dot_general | solution.py:46
  77.5 0.6 scatter.10
  78.1 0.6 scatter.11
  79.1 0.7 copy.100
  79.7 3.5 %all-to-all-start = ((f32[16,1,64]{2,1,0:T(1,128)}), f32[16,1,64]{2,1,0:T(1,128)S(1)}, u32[]{:S(2)}, u32[]{:S(2)}) async-start(f32[16,1,64]{2,1,0:T(1,128)} %copy.100), calls=%async_computation | async-start | bytes 16384 | tf_op jit(solution)/shard_map/all_to_all | solution.py:167
  83.6 0.7 and_reduce_fusion
  84.3 0.5 copy.118
  85.0 1.0 fusion.15
  85.9 0.7 fusion.19
  86.7 0.6 broadcast.203
  87.3 2.2 %reduce.30 = bf16[16,8192]{1,0:T(8,128)(2,1)S(1)} reduce(bf16[16,1,8192]{2,1,0:T(2,128)(2,1)S(1)} %reshape_reshape.8, bf16[]{:T(256)} %broadcast.203), dimensions={1}, to_apply=%reshape_reshape.8.reduce_sub_computation | reduce | bytes 524290 | tf_op jit(solution)/shard_map/reshape;reshape | solution.py:161
  89.5 0.9 reshape.327
  90.4 6.0 %all-to-all-start.1 = ((bf16[16,2,4096]{2,1,0:T(2,128)(2,1)}), bf16[16,2,4096]{2,1,0:T(2,128)(2,1)S(1)}, u32[]{:S(2)}, u32[]{:S(2)}) async-start(bf16[16,2,4096]{2,1,0:T(2,128)(2,1)} %reshape.327), calls=%async_computation.1 | async-start | bytes 524288 | tf_op jit(solution)/shard_map/all_to_all | solution.py:160
  96.5 9.9 %all-to-all-done.1 = bf16[16,2,4096]{2,1,0:T(2,128)(2,1)S(1)} async-done(((bf16[16,2,4096]{2,1,0:T(2,128)(2,1)}), bf16[16,2,4096]{2,1,0:T(2,128)(2,1)S(1)}, u32[]{:S(2)}, u32[]{:S(2)}) %all-to-all-start.1) | async-done | bytes 262176 | tf_op jit(solution)/shard_map/all_to_all | solution.py:160
  106.9 0.8 multiply_reduce_fusion
  107.8 0.7 divide_convert_fusion
  (76 shorter events, 4.8 us)
Async XLA Ops:
  7.3 0.8 copy-start.1
  7.3 27.0 %copy-start.7 = (s32[3]{0:T(128)S(1)}, s32[3]{0:T(128)}, u32[]{:S(2)}) copy-start(s32[3]{0:T(128)} %constant.101.clone.1) | copy-start | bytes 40
  7.9 30.4 %copy-start.5 = (bf16[1,2,1024]{2,1,0:T(2,128)(2,1)S(1)}, bf16[1,2,1024]{2,1,0:T(2,128)(2,1)}, u32[]{:S(2)}) copy-start(bf16[1,2,1024]{2,1,0:T(2,128)(2,1)} %param.17) | copy-start | bytes 12292
  49.7 27.8 %copy-start.4 = (f32[1,8,8]{0,2,1:T(8,128)S(1)}, f32[1,8,8]{0,2,1:T(8,128)}, u32[]{:S(2)}) copy-start(f32[1,8,8]{0,2,1:T(8,128)} %copy.96) | copy-start | bytes 772
  49.7 28.5 %copy-start.2 = (f32[1,8,8]{0,2,1:T(8,128)S(1)}, f32[1,8,8]{0,2,1:T(8,128)}, u32[]{:S(2)}) copy-start(f32[1,8,8]{0,2,1:T(8,128)} %copy.99) | copy-start | bytes 772
  49.7 29.1 %copy-start.3 = (f32[1,8,8]{0,2,1:T(8,128)S(1)}, f32[1,8,8]{0,2,1:T(8,128)}, u32[]{:S(2)}) copy-start(f32[1,8,8]{0,2,1:T(8,128)} %copy.97) | copy-start | bytes 772
  49.7 33.9 %copy-start.6 = (s32[4]{0:T(128)S(1)}, s32[4]{0:T(128)}, u32[]{:S(2)}) copy-start(s32[4]{0:T(128)} %constant.106.clone.1) | copy-start | bytes 52
  79.7 10.7 %all-to-all-start = ((f32[16,1,64]{2,1,0:T(1,128)}), f32[16,1,64]{2,1,0:T(1,128)S(1)}, u32[]{:S(2)}, u32[]{:S(2)}) async-start(f32[16,1,64]{2,1,0:T(1,128)} %copy.100), calls=%async_computation | async-start | bytes 16384 | tf_op jit(solution)/shard_map/all_to_all | solution.py:167
  84.3 1.6 %copy-start = (f32[8,128,128]{2,1,0:T(8,128)S(1)}, f32[8,128,128]{2,1,0:T(8,128)}, u32[]{:S(2)}) copy-start(f32[8,128,128]{2,1,0:T(8,128)} %get-tuple-element.82) | copy-start | bytes 1572868
  90.4 16.0 %all-to-all-start.1 = ((bf16[16,2,4096]{2,1,0:T(2,128)(2,1)}), bf16[16,2,4096]{2,1,0:T(2,128)(2,1)S(1)}, u32[]{:S(2)}, u32[]{:S(2)}) async-start(bf16[16,2,4096]{2,1,0:T(2,128)(2,1)} %reshape.327), calls=%async_computation.1 | async-start | bytes 524288 | tf_op jit(solution)/shard_map/all_to_all | solution.py:160
where the time goes:
time: 109 us; the launch traced here: 108 us
  matrix products  26.9 us (25%)
  blocking collectives  24.6 us (23%)
  local copies, waits for them, and re-layouts  22.6 us (21%)
  other arithmetic  12.5 us (11%)
  waiting for transfers between devices  9.93 us (9%)
  starting transfers between devices  9.44 us (9%)
  between operations  2.32 us (2%)
    all_gather x1, blocking collectives, per_device(): gathered_parts = lax.all_gather(queries, 'blk', axis=0, tiled=True)  24.6 us
    dot_general x8, matrix products, prefix_head(): jnp.dot(exponent.astype(jnp.bfloat16), values_block, preferred_element_ty...  14.9 us
    dot_general x8, matrix products, prefix_head(): jnp.dot(query_block, keys_block.T, preferred_element_type=jnp.float32)  9.99 us
    all_to_all x1, waiting for transfers between devices, per_device(): lax.all_to_all(normed_half.reshape(blocks, rows_per_block, QUERY_HEADS *...  9.93 us
    unnamed x23, local copies, waits for them, and re-layouts  9.02 us
    all_to_all x1, starting transfers between devices, per_device(): lax.all_to_all(normed_half.reshape(blocks, rows_per_block, QUERY_HEADS *...  5.97 us
    slice x1, local copies, waits for them, and re-layouts, per_device(): prefix_key_value[1]  3.96 us
    all_to_all x1, starting transfers between devices, per_device(): lax.all_to_all(lse.reshape(blocks, rows_per_block, QUERY_HEADS), 'blk', s...  3.47 us
  transfers between devices with their start and end apart: 2, of which 1 were waited for; matrix products, arithmetic and copies ran while one was open for 7% of the time, Pallas kernels for 0%

commit v1 on v0

--- a/solution.py
+++ b/solution.py
@@ -6,6 +6,24 @@
 QUERY_HEADS = 64
 KEY_VALUE_HEADS = 8
 HEAD_WIDTH = 128
+
+
+def laid_out(pieces, dim):
+    pieces = jnp.moveaxis(pieces, 0, dim)
+    shape = pieces.shape
+    return pieces.reshape(*shape[:dim], shape[dim] * shape[dim + 1], *shape[dim + 2 :])
+
+
+def grow_blocks(array, axis):
+    count = lax.axis_size(axis)
+    blocks = array[None]
+    for level in range(count.bit_length() - 1):
+        bit = 1 << level
+        other = lax.ppermute(blocks, axis, [(i, i ^ bit) for i in range(count)])
+        both = jnp.stack([blocks, other])
+        upper = lax.axis_index(axis) >> level & 1
+        blocks = jnp.where(upper == 0, both, both[::-1]).reshape(-1, *array.shape)
+    return blocks
 
 
 def per_device(queries, prefix_key_value, suffix_key_value, fresh_key_value, lengths, home):
@@ -17,7 +35,7 @@
     score_scale = HEAD_WIDTH ** (-0.5)
     prefix_length_count = prefix_key_value.shape[1]
     suffix_length_count = suffix_key_value.shape[2]
-    gathered_parts = lax.all_gather(queries, "blk", axis=0, tiled=True)
+    gathered_parts = laid_out(grow_blocks(queries, "blk"), 0)
     grouped_queries = gathered_parts.reshape(
         revision_count, KEY_VALUE_HEADS, query_group, HEAD_WIDTH
     )

time: 109 us -> 94.9 us (0.87)
  blocking collectives: 24.6 us -> 0 us
  starting transfers between devices: 9.44 us -> 17.4 us
  waiting for transfers between devices: 9.93 us -> 11.9 us
  local copies, waits for them, and re-layouts: 22.6 us -> 24.3 us
    all_gather x1 -> x0, blocking collectives: 24.6 us -> none  [per_device(): gathered_parts = lax.all_gather(queries, 'blk', axis=0, tiled=True)]
    ppermute x0 -> x4, starting transfers between devices: none -> 7.36 us  [grow_blocks(): other = lax.ppermute(blocks, axis, [(i, i ^ bit) for i in range(count)])]
    slice x1, local copies, waits for them, and re-layouts: 3.96 us -> 1.74 us  [per_device(): prefix_key_value[1]]
    ppermute x0 -> x4, waiting for transfers between devices: none -> 1.93 us  [grow_blocks(): other = lax.ppermute(blocks, axis, [(i, i ^ bit) for i in range(count)])]
    unnamed x23, local copies, waits for them, and re-layouts: 9.02 us -> 10.8 us
    rev x0 -> x1, local copies, waits for them, and re-layouts: none -> 1.65 us  [grow_blocks(): blocks = jnp.where(upper == 0, both, both[::-1]).reshape(-1, *array.shape)]
    all_gather x1 -> x0, other arithmetic: 1.52 us -> none  [per_device(): gathered_parts = lax.all_gather(queries, 'blk', axis=0, tiled=True)]
    slice x1, local copies, waits for them, and re-layouts: 1.71 us -> 3.17 us  [per_device(): suffix_key_value[:, 1]]
  transfers between devices with their start and end apart: 2 -> 6, of which waited for: 1 -> 2; matrix products, arithmetic and copies ran while one was open for 7% -> 28% of each run, Pallas kernels for 0% -> 0%
where the time goes in v1:
time: 94.9 us; the launch traced here: 94 us
  matrix products  26.4 us (28%)
  local copies, waits for them, and re-layouts  24.3 us (26%)
  starting transfers between devices  17.4 us (18%)
  waiting for transfers between devices  11.9 us (13%)
  other arithmetic  11.5 us (12%)
  between operations  2.38 us (3%)
    dot_general x8, matrix products, prefix_head(): jnp.dot(exponent.astype(jnp.bfloat16), values_block, preferred_element_ty...  14.9 us
    unnamed x23, local copies, waits for them, and re-layouts  10.8 us
    dot_general x8, matrix products, prefix_head(): jnp.dot(query_block, keys_block.T, preferred_element_type=jnp.float32)  9.99 us
    all_to_all x1, waiting for transfers between devices, per_device(): lax.all_to_all(normed_half.reshape(blocks, rows_per_block, QUERY_HEADS *...  9.93 us
    ppermute x4, starting transfers between devices, grow_blocks(): other = lax.ppermute(blocks, axis, [(i, i ^ bit) for i in range(count)])  7.36 us
    all_to_all x1, starting transfers between devices, per_device(): lax.all_to_all(normed_half.reshape(blocks, rows_per_block, QUERY_HEADS *...  6.01 us
    all_to_all x1, starting transfers between devices, per_device(): lax.all_to_all(lse.reshape(blocks, rows_per_block, QUERY_HEADS), 'blk', s...  4.02 us
    slice x1, local copies, waits for them, and re-layouts, per_device(): suffix_key_value[:, 1]  3.17 us
  transfers between devices with their start and end apart: 6, of which 2 were waited for; matrix products, arithmetic and copies ran while one was open for 28% of the time, Pallas kernels for 0%

profile of v1, /device:TPU:0, one launch (start us, length us, event | category | flops | bytes accessed | tf_op | source)
XLA Modules:
  0.0 94.0 jit_solution(9359751645434789923)
XLA Ops:
  0.5 3.2 %fusion.43 = (bf16[1,1,512,1024]{3,2,1,0:T(8,128)(2,1)}, bf16[1,1,512,1024]{3,2,1,0:T(8,128)(2,1)}) fusion(bf16[1,2,512,1024]{3,2,1,0:T(8,128)(2,1)} %param.16), kind=kLoop, calls=%fused_computation.73 | loop fusion | bytes 4194304 | tf_op jit(solution)/shard_map/slice | solution.py:89
  3.7 1.7 %fusion.42 = (bf16[1,1024,1024]{2,1,0:T(8,128)(2,1)S(1)}, bf16[1,1024,1024]{2,1,0:T(8,128)(2,1)}) fusion(bf16[2,1024,1024]{2,1,0:T(8,128)(2,1)S(1)} %copy-done), kind=kLoop, calls=%fused_computation.72 | loop fusion | bytes 8388608 | tf_op jit(solution)/shard_map/slice | solution.py:51
  5.7 0.9 broadcast.161.clone
  6.6 0.6 broadcast_dynamic-update-slice_fusion
  7.3 1.7 %rev.12 = bf16[2,1,1,8192]{3,0,2,1:T(2,128)(2,1)S(1)} reverse(bf16[2,1,1,8192]{3,0,2,1:T(2,128)(2,1)S(1)} %pad_maximum_fusion.3), dimensions={0} | reverse | bytes 65536 | tf_op jit(solution)/shard_map/rev | solution.py:25
  9.0 2.6 %collective-permute-start.1 = (bf16[2,1,8192]{2,0,1:T(2,128)(2,1)S(1)}, bf16[2,1,8192]{2,0,1:T(2,128)(2,1)S(1)}, u32[]{:S(2)}, u32[]{:S(2)}) collective-permute-start(bf16[2,1,8192]{2,0,1:T(2,128)(2,1)S(1)} %get-tuple-element.161), channel_id=1, source_target_pairs={{0,2},{1,3},{2,0},{3,1},{4,6},{5,7},{6,4},{7,5},{8,10},{9,11},{10,... | collective-permute-start | bytes 98312 | tf_op jit(solution)/shard_map/ppermute | solution.py:22
  11.6 0.6 fusion.37
  15.0 1.6 %collective-permute-start.2 = (bf16[4,1,8192]{2,0,1:T(4,128)(2,1)S(1)}, bf16[4,1,8192]{2,0,1:T(4,128)(2,1)S(1)}, u32[]{:S(2)}, u32[]{:S(2)}) collective-permute-start(bf16[4,1,8192]{2,0,1:T(4,128)(2,1)S(1)} %reshape.267), channel_id=1, source_target_pairs={{0,4},{1,5},{2,6},{3,7},{4,0},{5,1},{6,2},{7,3},{8,12},{9,13},{10,... | collective-permute-start | bytes 196616 | tf_op jit(solution)/shard_map/ppermute | solution.py:22
  16.6 0.7 and_reduce_fusion.1
  17.4 1.9 %collective-permute-done.2 = bf16[4,1,8192]{2,0,1:T(4,128)(2,1)S(1)} collective-permute-done((bf16[4,1,8192]{2,0,1:T(4,128)(2,1)S(1)}, bf16[4,1,8192]{2,0,1:T(4,128)(2,1)S(1)}, u32[]{:S(2)}, u32[]{:S(2)}) %collective-permute-start.2) | collective-permute-done | bytes 65568 | tf_op jit(solution)/shard_map/ppermute | solution.py:22
  19.5 2.7 %collective-permute-start.3 = (bf16[8,1,8192]{2,0,1:T(8,128)(2,1)S(1)}, bf16[8,1,8192]{2,0,1:T(8,128)(2,1)S(1)}, u32[]{:S(2)}, u32[]{:S(2)}) collective-permute-start(bf16[8,1,8192]{2,0,1:T(8,128)(2,1)S(1)} %reshape.268), channel_id=1, source_target_pairs={{0,8},{1,9},{2,10},{3,11},{4,12},{5,13},{6,14},{7,15},{8,0},{9,1},... | collective-permute-start | bytes 393224 | tf_op jit(solution)/shard_map/ppermute | solution.py:22
  22.2 0.6 iota_compare_fusion
  22.8 1.5 %copy.103 = bf16[1,1,512,1024]{2,3,1,0:T(8,128)(2,1)S(1)} copy(bf16[1,1,512,1024]{3,2,1,0:T(8,128)(2,1)} %get-tuple-element.159) | data formatting | bytes 2097152
  24.4 4.0 %copy.101 = bf16[1,1024,1024]{1,2,0:T(8,128)(2,1)} copy(bf16[1,1024,1024]{2,1,0:T(8,128)(2,1)} %get-tuple-element.157) | data formatting | bytes 4194304
  28.3 2.6 %copy.102 = bf16[1,1024,1024]{1,2,0:T(8,128)(2,1)} copy(bf16[1,1024,1024]{2,1,0:T(8,128)(2,1)S(1)} %get-tuple-element.156) | data formatting | bytes 4194304
  31.0 1.5 %copy.104 = bf16[1,1,512,1024]{2,3,1,0:T(8,128)(2,1)S(1)} copy(bf16[1,1,512,1024]{3,2,1,0:T(8,128)(2,1)} %get-tuple-element.158) | data formatting | bytes 2097152
  32.8 0.7 and_reduce_fusion
  34.2 0.6 select_bitcast_fusion
  35.1 27.4 %while.19 = (s32[]{:T(128)}, f32[8,128]{1,0:T(8,128)S(1)}, f32[8,128]{1,0:T(8,128)S(1)}, f32[8,128,128]{2,1,0:T(8,128)}, bf16[8,128,128]{2,1,0:T(8,128)(2,1)S(1)...) while((s32[]{:T(128)}, f32[8,128]{1,0:T(8,128)S(1)}, ...), condition=%wide.region_3.4_spmd, body=%wide.region_0.3_spmd.sunk | while | flops 67895040 | bytes 2201701 | solution.py:69
  35.2 1.2 %fusion.55 = (f32[128]{0:T(128)S(1)}, f32[128,1024]{1,0:T(8,128)S(1)}) fusion(bf16[8,1024,128]{1,2,0:T(8,128)(2,1)} %get-tuple-element.236, s32[]{:T(128)} %get-tuple-element.222, bf16[8,128,128]{2,1,0:T(8,128)(2,1)S(1)} %get-tuple-element.235), kind=kOutput, calls=%fused_computation.71.clone.1 | convolution fusion | flops 33816448 | bytes 820736 | tf_op jit(solution)/shard_map/while/body/eval_jaxpr/dot_general | solution.py:59
  36.4 1.9 %fusion.57 = f32[8,128,128]{2,1,0:T(8,128)} fusion(f32[8,128,128]{2,1,0:T(8,128)} %get-tuple-element.225, s32[]{:T(128)} %get-tuple-element.222, f32[128,1024]{1,0:T(8,128)S(1)} %get-tuple-element.212, bf16[8,1024,128]{1,2,0:T(8,128)(2,1)} %get-tuple-element.237, f32[128]{0:T(128)S(1)} %get-tuple-element.211), kind=kOutput, calls=%fused_computation.2.clone.1 | convolution fusion | flops 33816576 | bytes 853504 | tf_op jit(solution)/shard_map/while/body/eval_jaxpr/dot_general | solution.py:64
  38.6 1.2 %fusion.55 = (f32[128]{0:T(128)S(1)}, f32[128,1024]{1,0:T(8,128)S(1)}) fusion(bf16[8,1024,128]{1,2,0:T(8,128)(2,1)} %get-tuple-element.236, s32[]{:T(128)} %get-tuple-element.222, bf16[8,128,128]{2,1,0:T(8,128)(2,1)S(1)} %get-tuple-element.235), kind=kOutput, calls=%fused_computation.71.clone.1 | convolution fusion | flops 33816448 | bytes 820736 | tf_op jit(solution)/shard_map/while/body/eval_jaxpr/dot_general | solution.py:59
  39.8 1.9 %fusion.57 = f32[8,128,128]{2,1,0:T(8,128)} fusion(f32[8,128,128]{2,1,0:T(8,128)} %get-tuple-element.225, s32[]{:T(128)} %get-tuple-element.222, f32[128,1024]{1,0:T(8,128)S(1)} %get-tuple-element.212, bf16[8,1024,128]{1,2,0:T(8,128)(2,1)} %get-tuple-element.237, f32[128]{0:T(128)S(1)} %get-tuple-element.211), kind=kOutput, calls=%fused_computation.2.clone.1 | convolution fusion | flops 33816576 | bytes 853504 | tf_op jit(solution)/shard_map/while/body/eval_jaxpr/dot_general | solution.py:64
  42.0 1.2 %fusion.55 = (f32[128]{0:T(128)S(1)}, f32[128,1024]{1,0:T(8,128)S(1)}) fusion(bf16[8,1024,128]{1,2,0:T(8,128)(2,1)} %get-tuple-element.236, s32[]{:T(128)} %get-tuple-element.222, bf16[8,128,128]{2,1,0:T(8,128)(2,1)S(1)} %get-tuple-element.235), kind=kOutput, calls=%fused_computation.71.clone.1 | convolution fusion | flops 33816448 | bytes 820736 | tf_op jit(solution)/shard_map/while/body/eval_jaxpr/dot_general | solution.py:59
  43.3 1.9 %fusion.57 = f32[8,128,128]{2,1,0:T(8,128)} fusion(f32[8,128,128]{2,1,0:T(8,128)} %get-tuple-element.225, s32[]{:T(128)} %get-tuple-element.222, f32[128,1024]{1,0:T(8,128)S(1)} %get-tuple-element.212, bf16[8,1024,128]{1,2,0:T(8,128)(2,1)} %get-tuple-element.237, f32[128]{0:T(128)S(1)} %get-tuple-element.211), kind=kOutput, calls=%fused_computation.2.clone.1 | convolution fusion | flops 33816576 | bytes 853504 | tf_op jit(solution)/shard_map/while/body/eval_jaxpr/dot_general | solution.py:64
  45.4 1.2 %fusion.55 = (f32[128]{0:T(128)S(1)}, f32[128,1024]{1,0:T(8,128)S(1)}) fusion(bf16[8,1024,128]{1,2,0:T(8,128)(2,1)} %get-tuple-element.236, s32[]{:T(128)} %get-tuple-element.222, bf16[8,128,128]{2,1,0:T(8,128)(2,1)S(1)} %get-tuple-element.235), kind=kOutput, calls=%fused_computation.71.clone.1 | convolution fusion | flops 33816448 | bytes 820736 | tf_op jit(solution)/shard_map/while/body/eval_jaxpr/dot_general | solution.py:59
  46.7 1.9 %fusion.57 = f32[8,128,128]{2,1,0:T(8,128)} fusion(f32[8,128,128]{2,1,0:T(8,128)} %get-tuple-element.225, s32[]{:T(128)} %get-tuple-element.222, f32[128,1024]{1,0:T(8,128)S(1)} %get-tuple-element.212, bf16[8,1024,128]{1,2,0:T(8,128)(2,1)} %get-tuple-element.237, f32[128]{0:T(128)S(1)} %get-tuple-element.211), kind=kOutput, calls=%fused_computation.2.clone.1 | convolution fusion | flops 33816576 | bytes 853504 | tf_op jit(solution)/shard_map/while/body/eval_jaxpr/dot_general | solution.py:64
  48.9 1.2 %fusion.55 = (f32[128]{0:T(128)S(1)}, f32[128,1024]{1,0:T(8,128)S(1)}) fusion(bf16[8,1024,128]{1,2,0:T(8,128)(2,1)} %get-tuple-element.236, s32[]{:T(128)} %get-tuple-element.222, bf16[8,128,128]{2,1,0:T(8,128)(2,1)S(1)} %get-tuple-element.235), kind=kOutput, calls=%fused_computation.71.clone.1 | convolution fusion | flops 33816448 | bytes 820736 | tf_op jit(solution)/shard_map/while/body/eval_jaxpr/dot_general | solution.py:59
  50.1 1.9 %fusion.57 = f32[8,128,128]{2,1,0:T(8,128)} fusion(f32[8,128,128]{2,1,0:T(8,128)} %get-tuple-element.225, s32[]{:T(128)} %get-tuple-element.222, f32[128,1024]{1,0:T(8,128)S(1)} %get-tuple-element.212, bf16[8,1024,128]{1,2,0:T(8,128)(2,1)} %get-tuple-element.237, f32[128]{0:T(128)S(1)} %get-tuple-element.211), kind=kOutput, calls=%fused_computation.2.clone.1 | convolution fusion | flops 33816576 | bytes 853504 | tf_op jit(solution)/shard_map/while/body/eval_jaxpr/dot_general | solution.py:64
  52.3 1.2 %fusion.55 = (f32[128]{0:T(128)S(1)}, f32[128,1024]{1,0:T(8,128)S(1)}) fusion(bf16[8,1024,128]{1,2,0:T(8,128)(2,1)} %get-tuple-element.236, s32[]{:T(128)} %get-tuple-element.222, bf16[8,128,128]{2,1,0:T(8,128)(2,1)S(1)} %get-tuple-element.235), kind=kOutput, calls=%fused_computation.71.clone.1 | convolution fusion | flops 33816448 | bytes 820736 | tf_op jit(solution)/shard_map/while/body/eval_jaxpr/dot_general | solution.py:59
  53.5 1.9 %fusion.57 = f32[8,128,128]{2,1,0:T(8,128)} fusion(f32[8,128,128]{2,1,0:T(8,128)} %get-tuple-element.225, s32[]{:T(128)} %get-tuple-element.222, f32[128,1024]{1,0:T(8,128)S(1)} %get-tuple-element.212, bf16[8,1024,128]{1,2,0:T(8,128)(2,1)} %get-tuple-element.237, f32[128]{0:T(128)S(1)} %get-tuple-element.211), kind=kOutput, calls=%fused_computation.2.clone.1 | convolution fusion | flops 33816576 | bytes 853504 | tf_op jit(solution)/shard_map/while/body/eval_jaxpr/dot_general | solution.py:64
  55.7 1.2 %fusion.55 = (f32[128]{0:T(128)S(1)}, f32[128,1024]{1,0:T(8,128)S(1)}) fusion(bf16[8,1024,128]{1,2,0:T(8,128)(2,1)} %get-tuple-element.236, s32[]{:T(128)} %get-tuple-element.222, bf16[8,128,128]{2,1,0:T(8,128)(2,1)S(1)} %get-tuple-element.235), kind=kOutput, calls=%fused_computation.71.clone.1 | convolution fusion | flops 33816448 | bytes 820736 | tf_op jit(solution)/shard_map/while/body/eval_jaxpr/dot_general | solution.py:59
  57.0 1.9 %fusion.57 = f32[8,128,128]{2,1,0:T(8,128)} fusion(f32[8,128,128]{2,1,0:T(8,128)} %get-tuple-element.225, s32[]{:T(128)} %get-tuple-element.222, f32[128,1024]{1,0:T(8,128)S(1)} %get-tuple-element.212, bf16[8,1024,128]{1,2,0:T(8,128)(2,1)} %get-tuple-element.237, f32[128]{0:T(128)S(1)} %get-tuple-element.211), kind=kOutput, calls=%fused_computation.2.clone.1 | convolution fusion | flops 33816576 | bytes 853504 | tf_op jit(solution)/shard_map/while/body/eval_jaxpr/dot_general | solution.py:64
  59.1 1.3 %fusion.55 = (f32[128]{0:T(128)S(1)}, f32[128,1024]{1,0:T(8,128)S(1)}) fusion(bf16[8,1024,128]{1,2,0:T(8,128)(2,1)} %get-tuple-element.236, s32[]{:T(128)} %get-tuple-element.222, bf16[8,128,128]{2,1,0:T(8,128)(2,1)S(1)} %get-tuple-element.235), kind=kOutput, calls=%fused_computation.71.clone.1 | convolution fusion | flops 33816448 | bytes 820736 | tf_op jit(solution)/shard_map/while/body/eval_jaxpr/dot_general | solution.py:59
  60.4 1.9 %fusion.57 = f32[8,128,128]{2,1,0:T(8,128)} fusion(f32[8,128,128]{2,1,0:T(8,128)} %get-tuple-element.225, s32[]{:T(128)} %get-tuple-element.222, f32[128,1024]{1,0:T(8,128)S(1)} %get-tuple-element.212, bf16[8,1024,128]{1,2,0:T(8,128)(2,1)} %get-tuple-element.237, f32[128]{0:T(128)S(1)} %get-tuple-element.211), kind=kOutput, calls=%fused_computation.2.clone.1 | convolution fusion | flops 33816576 | bytes 853504 | tf_op jit(solution)/shard_map/while/body/eval_jaxpr/dot_general | solution.py:64
  62.9 0.6 scatter.10
  63.5 0.6 scatter.11
  64.6 0.7 copy.86
  65.3 4.0 %all-to-all-start = ((f32[16,1,64]{2,1,0:T(1,128)}), f32[16,1,64]{2,1,0:T(1,128)S(1)}, u32[]{:S(2)}, u32[]{:S(2)}) async-start(f32[16,1,64]{2,1,0:T(1,128)} %copy.86), calls=%async_computation | async-start | bytes 16384 | tf_op jit(solution)/shard_map/all_to_all | solution.py:185
  69.3 1.0 %fusion.15 = f32[16,8,8,128]{3,2,1,0:T(8,128)S(1)} fusion(f32[16,8,8,128]{3,2,1,0:T(8,128)S(1)} %broadcast.161.clone.1, s32[]{:T(128)} %bitcast.23, bf16[512,8,128]{0,2,1:T(8,128)(2,1)S(1)} %bitcast.140, f32[8,8,512]{2,1,0:T(8,128)S(1)} %get-tuple-element.163, f32[8,8]{1,0:T(8,128)S(1)} %get-tuple-element.162, pred[]{:T(512)} %and_reduce_fusion), kind=kOutput, calls=%fused_computation.19 | convolution fusion | flops 8462336 | bytes 1216517 | tf_op jit(solution)/shard_map/rhgt,rthd->rhgd/dot_general | solution.py:105
  70.4 1.7 %fusion.19 = bf16[16,8,8,128]{3,2,1,0:T(8,128)(2,1)S(1)} fusion(f32[16,8,8,128]{3,2,1,0:T(8,128)} %broadcast_dynamic-update-slice_fusion, f32[16,8,8,128]{3,2,1,0:T(8,128)S(1)} %fusion.15, f32[16,8,8]{2,1,0:T(8,128)S(1)} %copy.93, f32[16,8,8]{2,1,0:T(8,128)S(1)} %copy.92, f32[16,8,8]{2,1,0:T(8,128)S(1)} %copy.89, f32[16,8,8]{2,1,0:T(8,128)S(1)} %copy.87, ...), kind=kLoop, calls=%fused_computation.25 | loop fusion | flops 917504 | bytes 1851392 | tf_op jit(solution)/shard_map/convert_element_type | solution.py:174
  72.2 0.6 broadcast.202
  72.8 2.2 %reduce.29 = bf16[16,8192]{1,0:T(8,128)(2,1)S(1)} reduce(bf16[16,1,8192]{2,1,0:T(2,128)(2,1)S(1)} %reshape_reshape.8, bf16[]{:T(256)} %broadcast.202), dimensions={1}, to_apply=%reshape_reshape.8.reduce_sub_computation | reduce | bytes 524290 | tf_op jit(solution)/shard_map/reshape;reshape | solution.py:179
  75.0 0.9 reshape.331
  75.9 6.0 %all-to-all-start.1 = ((bf16[16,2,4096]{2,1,0:T(2,128)(2,1)}), bf16[16,2,4096]{2,1,0:T(2,128)(2,1)S(1)}, u32[]{:S(2)}, u32[]{:S(2)}) async-start(bf16[16,2,4096]{2,1,0:T(2,128)(2,1)} %reshape.331), calls=%async_computation.1 | async-start | bytes 524288 | tf_op jit(solution)/shard_map/all_to_all | solution.py:178
  82.0 9.9 %all-to-all-done.1 = bf16[16,2,4096]{2,1,0:T(2,128)(2,1)S(1)} async-done(((bf16[16,2,4096]{2,1,0:T(2,128)(2,1)}), bf16[16,2,4096]{2,1,0:T(2,128)(2,1)S(1)}, u32[]{:S(2)}, u32[]{:S(2)}) %all-to-all-start.1) | async-done | bytes 262176 | tf_op jit(solution)/shard_map/all_to_all | solution.py:178
  92.4 0.8 multiply_reduce_fusion
  93.3 0.7 divide_convert_fusion
  (95 shorter events, 7.1 us)
Async XLA Ops:
  0.0 7.2 %collective-permute-start = (bf16[1,1,8192]{2,1,0:T(2,128)(2,1)}, bf16[1,1,8192]{2,1,0:T(2,128)(2,1)S(1)}, u32[]{:S(2)}, u32[]{:S(2)}) collective-permute-start(bf16[1,1,8192]{2,1,0:T(2,128)(2,1)} %bitcast.146), channel_id=1, source_target_pairs={{0,1},{1,0},{2,3},{3,2},{4,5},{5,4},{6,7},{7,6},{8,9},{9,8},{10,11... | collective-permute-start | bytes 49160 | tf_op jit(solution)/shard_map/ppermute | solution.py:22
  0.5 3.2 %copy-start = (bf16[2,1024,1024]{2,1,0:T(8,128)(2,1)S(1)}, bf16[2,1024,1024]{2,1,0:T(8,128)(2,1)}, u32[]{:S(2)}) copy-start(bf16[2,1024,1024]{2,1,0:T(8,128)(2,1)} %param.15) | copy-start | bytes 12582916
  3.7 1.8 %copy-start.2 = (bf16[1,8192]{1,0:T(2,128)(2,1)S(1)}, bf16[1,8192]{1,0:T(2,128)(2,1)}, u32[]{:S(2)}) copy-start(bf16[1,8192]{1,0:T(2,128)(2,1)} %param.14) | copy-start | bytes 49156
  3.7 1.9 %copy-start.3 = (bf16[1,2,1024]{2,1,0:T(2,128)(2,1)S(1)}, bf16[1,2,1024]{2,1,0:T(2,128)(2,1)}, u32[]{:S(2)}) copy-start(bf16[1,2,1024]{2,1,0:T(2,128)(2,1)} %param.17) | copy-start | bytes 12292
  3.7 7.9 %copy-start.6 = (s32[16]{0:T(128)S(1)}, s32[16]{0:T(128)}, u32[]{:S(2)}) copy-start(s32[16]{0:T(128)} %param.19) | copy-start | bytes 196
  3.7 10.5 %copy-start.7 = (s32[16]{0:T(128)S(1)}, s32[16]{0:T(128)}, u32[]{:S(2)}) copy-start(s32[16]{0:T(128)} %param.18) | copy-start | bytes 196
  3.7 12.9 %copy-start.5 = (s32[3]{0:T(128)S(1)}, s32[3]{0:T(128)}, u32[]{:S(2)}) copy-start(s32[3]{0:T(128)} %constant.107.clone.1) | copy-start | bytes 40
  9.0 5.7 %collective-permute-start.1 = (bf16[2,1,8192]{2,0,1:T(2,128)(2,1)S(1)}, bf16[2,1,8192]{2,0,1:T(2,128)(2,1)S(1)}, u32[]{:S(2)}, u32[]{:S(2)}) collective-permute-start(bf16[2,1,8192]{2,0,1:T(2,128)(2,1)S(1)} %get-tuple-element.161), channel_id=1, source_target_pairs={{0,2},{1,3},{2,0},{3,1},{4,6},{5,7},{6,4},{7,5},{8,10},{9,11},{10,... | collective-permute-start | bytes 98312 | tf_op jit(solution)/shard_map/ppermute | solution.py:22
  15.0 4.3 %collective-permute-start.2 = (bf16[4,1,8192]{2,0,1:T(4,128)(2,1)S(1)}, bf16[4,1,8192]{2,0,1:T(4,128)(2,1)S(1)}, u32[]{:S(2)}, u32[]{:S(2)}) collective-permute-start(bf16[4,1,8192]{2,0,1:T(4,128)(2,1)S(1)} %reshape.267), channel_id=1, source_target_pairs={{0,4},{1,5},{2,6},{3,7},{4,0},{5,1},{6,2},{7,3},{8,12},{9,13},{10,... | collective-permute-start | bytes 196616 | tf_op jit(solution)/shard_map/ppermute | solution.py:22
  19.5 14.0 %collective-permute-start.3 = (bf16[8,1,8192]{2,0,1:T(8,128)(2,1)S(1)}, bf16[8,1,8192]{2,0,1:T(8,128)(2,1)S(1)}, u32[]{:S(2)}, u32[]{:S(2)}) collective-permute-start(bf16[8,1,8192]{2,0,1:T(8,128)(2,1)S(1)} %reshape.268), channel_id=1, source_target_pairs={{0,8},{1,9},{2,10},{3,11},{4,12},{5,13},{6,14},{7,15},{8,0},{9,1},... | collective-permute-start | bytes 393224 | tf_op jit(solution)/shard_map/ppermute | solution.py:22
  30.9 1.9 %copy-start.4 = (s32[4]{0:T(128)S(1)}, s32[4]{0:T(128)}, u32[]{:S(2)}) copy-start(s32[4]{0:T(128)} %constant.112.clone.1) | copy-start | bytes 52
  62.6 7.8 %copy-start.1 = (f32[8,128,128]{2,1,0:T(8,128)S(1)}, f32[8,128,128]{2,1,0:T(8,128)}, u32[]{:S(2)}) copy-start(f32[8,128,128]{2,1,0:T(8,128)} %get-tuple-element.82) | copy-start | bytes 1572868
  65.3 10.6 %all-to-all-start = ((f32[16,1,64]{2,1,0:T(1,128)}), f32[16,1,64]{2,1,0:T(1,128)S(1)}, u32[]{:S(2)}, u32[]{:S(2)}) async-start(f32[16,1,64]{2,1,0:T(1,128)} %copy.86), calls=%async_computation | async-start | bytes 16384 | tf_op jit(solution)/shard_map/all_to_all | solution.py:185
  75.9 16.0 %all-to-all-start.1 = ((bf16[16,2,4096]{2,1,0:T(2,128)(2,1)}), bf16[16,2,4096]{2,1,0:T(2,128)(2,1)S(1)}, u32[]{:S(2)}, u32[]{:S(2)}) async-start(bf16[16,2,4096]{2,1,0:T(2,128)(2,1)} %reshape.331), calls=%async_computation.1 | async-start | bytes 524288 | tf_op jit(solution)/shard_map/all_to_all | solution.py:178
